TPU v7x, 32 devices: a whole 2x2x4 slice. The times are simulated.
32 devices in a mesh: dp: 8 (over z, y), mp: 4 (over x, core).
Axes of the slice: x: 2, y: 2, z: 4, core: 2. Of those that a mesh axis runs over, the one named last changes fastest.
Arguments:
- tokens: bfloat16 [8192, 2048], P('dp'), may hold values from -6 to 6
- out_cot: bfloat16 [8192, 2048], P('dp'), may hold values from -23 to 23
- lengths: int32 [8], P('dp'), may hold values from 1 to 1024, 6144 in all
- seq_family: int32 [8, 1], P('dp'), may hold values from 0 to 3
- family_tokens: int32 [4], replicated, may hold values from 100000 to 3999999
- norm_master: float32 [2048, 6], P('dp'), may hold values from -0.5 to 2.4, as said below
- attn_bias_master: float32 [2, 2048], P(None, 'mp'), may hold values from -2 to 2
- qkv_master: float32 [2048, 3, 2048], P('dp', None, 'mp'), may hold values from -0.125 to 0.125
- proj_master: float32 [2048, 2048], P('dp', 'mp'), may hold values from -1.5 to 1.5
- fc_bias_master: float32 [8192], P('mp'), may hold values from -1.5 to 1.5
- fc_master: float32 [2048, 8192], P('dp', 'mp'), may hold values from -0.125 to 0.125
- down_master: float32 [2048, 8192], P('dp', 'mp'), may hold values from -0.0625 to 0.0625
- norm_moment: float32 [2048, 6], P('dp'), may hold values from -0.0008544922 to 0.0008544922
- attn_bias_moment: float32 [2, 2048], P(None, 'mp'), may hold values from -0.0008544922 to 0.0008544922
- qkv_moment: float32 [2048, 3, 2048], P('dp', None, 'mp'), may hold values from -0.0008544922 to 0.0008544922
- proj_moment: float32 [2048, 2048], P('dp', 'mp'), may hold values from -0.0008544922 to 0.0008544922
- fc_bias_moment: float32 [8192], P('mp'), may hold values from -0.0008544922 to 0.0008544922
- fc_moment: float32 [2048, 8192], P('dp', 'mp'), may hold values from -0.0008544922 to 0.0008544922
- down_moment: float32 [2048, 8192], P('dp', 'mp'), may hold values from -0.0008544922 to 0.0008544922
- norm_average: float32 [2048, 6], P('dp'), may hold values from 0.5 to 1.5
- attn_bias_average: float32 [2, 2048], P(None, 'mp'), may hold values from -2 to 2
- qkv_average: float32 [2048, 3, 2048], P('dp', None, 'mp'), may hold values from -0.125 to 0.125
- proj_average: float32 [2048, 2048], P('dp', 'mp'), may hold values from -1.5 to 1.5
- fc_bias_average: float32 [8192], P('mp'), may hold values from -1.5 to 1.5
- fc_average: float32 [2048, 8192], P('dp', 'mp'), may hold values from -0.125 to 0.125
- down_average: float32 [2048, 8192], P('dp', 'mp'), may hold values from -0.0625 to 0.0625
Outputs:
- block_out: bfloat16 [8192, 2048], P('dp')
- input_grad: float32 [8192, 2048], P('dp')
- norm_grad: float32 [2048, 6], P('dp')
- attn_bias_grad: float32 [2, 2048], P(None, 'mp')
- qkv_grad: float32 [2048, 3, 2048], P('dp', None, 'mp')
- proj_grad: float32 [2048, 2048], P('dp', 'mp')
- fc_bias_grad: float32 [8192], P('mp')
- fc_grad: float32 [2048, 8192], P('dp', 'mp')
- down_grad: float32 [2048, 8192], P('dp', 'mp')
- norm_momentum: float32 [2048, 6], P('dp')
- attn_bias_momentum: float32 [2, 2048], P(None, 'mp')
- qkv_momentum: float32 [2048, 3, 2048], P('dp', None, 'mp')
- proj_momentum: float32 [2048, 2048], P('dp', 'mp')
- fc_bias_momentum: float32 [8192], P('mp')
- fc_momentum: float32 [2048, 8192], P('dp', 'mp')
- down_momentum: float32 [2048, 8192], P('dp', 'mp')
- norm_averaged: float32 [2048, 6], P('dp')
- attn_bias_averaged: float32 [2, 2048], P(None, 'mp')
- qkv_averaged: float32 [2048, 3, 2048], P('dp', None, 'mp')
- proj_averaged: float32 [2048, 2048], P('dp', 'mp')
- fc_bias_averaged: float32 [8192], P('mp')
- fc_averaged: float32 [2048, 8192], P('dp', 'mp')
- down_averaged: float32 [2048, 8192], P('dp', 'mp')
- norm_updated: float32 [2048, 6], P('dp')
- attn_bias_updated: float32 [2, 2048], P(None, 'mp')
- qkv_updated: float32 [2048, 3, 2048], P('dp', None, 'mp')
- proj_updated: float32 [2048, 2048], P('dp', 'mp')
- fc_bias_updated: float32 [8192], P('mp')
- fc_updated: float32 [2048, 8192], P('dp', 'mp')
- down_updated: float32 [2048, 8192], P('dp', 'mp')
- norm_copy: bfloat16 [2048, 6], P('dp')
- attn_bias_copy: bfloat16 [2, 2048], P(None, 'mp')
- qkv_copy: bfloat16 [2048, 3, 2048], P('dp', None, 'mp')
- proj_copy: bfloat16 [2048, 2048], P('dp', 'mp')
- fc_bias_copy: bfloat16 [8192], P('mp')
- fc_copy: bfloat16 [2048, 8192], P('dp', 'mp')
- down_copy: bfloat16 [2048, 8192], P('dp', 'mp')
- grad_norm: float32 [], replicated
Inputs may be any that keep to these rules, and one draw needn't show every extreme that they name: `lengths`: they sum to 6144; the longest is 1024. `seq_family`: every family has a sequence. `norm_master`: gains positive, biases of either sign.
All inputs are finite; a program needn't handle non-finite values. No bound on the sum of `lengths` on one device may be relied on, other than what follows from the above.
Results may differ from a plain program's by a relative error of at most 0.012.
The roundings to bfloat16 on the way count: a program that leaves them out, or rounds other values in their place, can miss the bound.
Values may be sent and summed in bfloat16 or wider, within the bound.
A program may use at most 256 MiB of HBM per device.

v0:
```python
import math
import jax
import jax.numpy as jnp
from jax import lax
from jax.sharding import PartitionSpec as P

HEAD_DIM = 128
LEN = 1024
EPS = 1e-05
MOMENTUM = 0.9
RATE = 192.0
KEEP = 0.9
NEG = -1e30


def layer_norm(value, gain, shift):
    centre = jnp.mean(value, axis=-1, keepdims=True)
    centred = value - centre
    spread = jnp.mean(centred * centred, axis=-1, keepdims=True)
    return centred * lax.rsqrt(spread + EPS) * gain + shift


def gelu_tanh(value):
    return (
        0.5
        * value
        * (1.0 + jnp.tanh(0.7978845608028654 * (value + 0.044715 * value * value * value)))
    )


def local(
    tokens,
    out_cot,
    lengths,
    seq_family,
    family_tokens,
    norm_master,
    attn_bias_master,
    qkv_master,
    proj_master,
    fc_bias_master,
    fc_master,
    down_master,
    norm_moment,
    attn_bias_moment,
    qkv_moment,
    proj_moment,
    fc_bias_moment,
    fc_moment,
    down_moment,
    norm_average,
    attn_bias_average,
    qkv_average,
    proj_average,
    fc_bias_average,
    fc_average,
    down_average,
):
    seq_count = lengths.shape[0]
    row_count = tokens.shape[0]
    seq_len = row_count // seq_count
    family_count = family_tokens.shape[0]
    local_heads = qkv_master.shape[2] // HEAD_DIM
    head_width = qkv_master.shape[2]
    scale = 1.0 / math.sqrt(HEAD_DIM)
    mp_count = lax.axis_size("mp")
    dp_count = lax.axis_size("dp")

    def sum_over_mp(term_fn):
        summed = lax.psum(term_fn(0, row_count), "mp")
        return summed

    family_ids = jnp.arange(family_count, dtype=jnp.int32)
    member = seq_family == family_ids[None, :]
    local_counts = jnp.sum(jnp.where(member, lengths[:, None], 0), axis=0).astype(jnp.float32)
    counts = lax.psum(local_counts, "dp")
    valid_total = jnp.sum(counts)
    share = family_tokens.astype(jnp.float32) / jnp.sum(family_tokens).astype(jnp.float32)
    family_weight = share * valid_total / jnp.maximum(counts, float(LEN // 2))
    seq_weight = jnp.sum(jnp.where(member, family_weight[None, :], 0.0), axis=1)
    places = jnp.arange(seq_len, dtype=jnp.int32)
    token_weight = jnp.where(places[None, :] < lengths[:, None], seq_weight[:, None], 0.0).reshape(
        row_count
    )
    causal = places[:, None] >= places[None, :]
    low_norm = norm_master.astype(jnp.bfloat16)
    low_qkv = qkv_master.astype(jnp.bfloat16)
    low_proj = proj_master.astype(jnp.bfloat16)
    low_fc = fc_master.astype(jnp.bfloat16)
    low_down = down_master.astype(jnp.bfloat16)
    w_qkv, w_proj, w_fc, w_down, w_norm = (
        lax.all_gather(low_qkv, "dp", axis=0, tiled=True),
        lax.all_gather(low_proj, "dp", axis=0, tiled=True),
        lax.all_gather(low_fc, "dp", axis=0, tiled=True),
        lax.all_gather(low_down, "dp", axis=0, tiled=True),
        lax.all_gather(low_norm, "dp", axis=0, tiled=True),
    )
    norm_full = w_norm.astype(jnp.float32)
    bias_rows = jnp.stack(
        [attn_bias_master[0], jnp.zeros_like(attn_bias_master[0]), attn_bias_master[1]], axis=0
    )
    x_in = tokens.astype(jnp.float32)
    ln1_low = layer_norm(x_in, norm_full[:, 0], norm_full[:, 1]).astype(jnp.bfloat16)
    qkv = (
        jnp.einsum("td,dce->tce", ln1_low, w_qkv, preferred_element_type=jnp.float32)
        + bias_rows[None]
    )
    qkv = qkv.astype(jnp.bfloat16)
    heads = qkv.reshape(seq_count, seq_len, 3, local_heads, HEAD_DIM)

    def attend(one_seq):
        query_rows = one_seq[:, 0]
        key_rows = one_seq[:, 1]
        value_rows = one_seq[:, 2]
        scores = (
            jnp.einsum("qhd,khd->hqk", query_rows, key_rows, preferred_element_type=jnp.float32)
            * scale
        )
        scores = jnp.where(causal[None], scores, NEG)
        row_top = jnp.max(scores, axis=-1, keepdims=True)
        log_total = row_top + jnp.log(jnp.sum(jnp.exp(scores - row_top), axis=-1, keepdims=True))
        attn_prob = jnp.exp(scores - log_total).astype(jnp.bfloat16)
        mixed = jnp.einsum(
            "hqk,khd->qhd", attn_prob, value_rows, preferred_element_type=jnp.float32
        )
        return (mixed.astype(jnp.bfloat16), log_total)

    mixed_low, log_kept = lax.map(attend, heads)
    mixed_low = mixed_low.reshape(row_count, head_width)

    def attn_term(start, count):
        return jnp.einsum("te,de->td", mixed_low, w_proj, preferred_element_type=jnp.float32)

    residual_part = x_in + sum_over_mp(attn_term) + norm_full[:, 4]
    ln2_part, ln2_back = jax.vjp(layer_norm, residual_part, norm_full[:, 2], norm_full[:, 3])
    ln2_low = ln2_part.astype(jnp.bfloat16)
    pre_act = (
        jnp.einsum("td,df->tf", ln2_low, w_fc, preferred_element_type=jnp.float32)
        + fc_bias_master[None]
    )
    hidden_act, gelu_back = jax.vjp(gelu_tanh, pre_act)
    hidden_low = hidden_act.astype(jnp.bfloat16)

    def mlp_term(start, count):
        return jnp.einsum("tf,df->td", hidden_low, w_down, preferred_element_type=jnp.float32)

    block_part = (residual_part + sum_over_mp(mlp_term) + norm_full[:, 5]).astype(jnp.bfloat16)
    upstream = token_weight[:, None] * out_cot.astype(jnp.float32)
    upstream_low = upstream.astype(jnp.bfloat16)
    down_sum = jnp.einsum("td,tf->df", upstream_low, hidden_low, preferred_element_type=jnp.float32)
    back_act = jnp.einsum("td,df->tf", upstream_low, w_down, preferred_element_type=jnp.float32)
    back_pre = gelu_back(back_act)[0].astype(jnp.bfloat16)
    fc_bias_sum = jnp.sum(back_pre, axis=0, dtype=jnp.float32)
    fc_sum = jnp.einsum("td,tf->df", ln2_low, back_pre, preferred_element_type=jnp.float32)

    def fc_back_term(start, count):
        return jnp.einsum("tf,df->td", back_pre, w_fc, preferred_element_type=jnp.float32)

    back_ln2 = sum_over_mp(fc_back_term)
    back_resid_part, gain2_sum, shift2_sum = ln2_back(back_ln2)
    back_resid_part = upstream + back_resid_part
    back_attn_low = back_resid_part.astype(jnp.bfloat16)
    proj_sum = jnp.einsum("td,te->de", back_attn_low, mixed_low, preferred_element_type=jnp.float32)
    back_mixed = jnp.einsum(
        "td,de->te", back_attn_low, w_proj, preferred_element_type=jnp.float32
    ).astype(jnp.bfloat16)
    back_mixed = back_mixed.reshape(seq_count, seq_len, local_heads, HEAD_DIM)

    def attend_back(items):
        one_seq, log_total, back_seq = items
        query_rows = one_seq[:, 0]
        key_rows = one_seq[:, 1]
        value_rows = one_seq[:, 2]
        scores = (
            jnp.einsum("qhd,khd->hqk", query_rows, key_rows, preferred_element_type=jnp.float32)
            * scale
        )
        scores = jnp.where(causal[None], scores, NEG)
        attn_prob = jnp.exp(scores - log_total)
        prob_low = attn_prob.astype(jnp.bfloat16)
        back_value = jnp.einsum(
            "hqk,qhd->khd", prob_low, back_seq, preferred_element_type=jnp.float32
        )
        back_prob = jnp.einsum(
            "qhd,khd->hqk", back_seq, value_rows, preferred_element_type=jnp.float32
        )
        back_score = attn_prob * (
            back_prob - jnp.sum(attn_prob * back_prob, axis=-1, keepdims=True)
        )
        back_score = back_score.astype(jnp.bfloat16)
        back_query = (
            jnp.einsum("hqk,khd->qhd", back_score, key_rows, preferred_element_type=jnp.float32)
            * scale
        )
        back_key = (
            jnp.einsum("hqk,qhd->khd", back_score, query_rows, preferred_element_type=jnp.float32)
            * scale
        )
        return jnp.stack([back_query, back_key, back_value], axis=1).astype(jnp.bfloat16)

    back_heads = lax.map(attend_back, (heads, log_kept, back_mixed))
    back_qkv = back_heads.reshape(row_count, 3, head_width)
    attn_bias_sum = jnp.sum(back_qkv[:, 0::2], axis=0, dtype=jnp.float32)
    qkv_sum = jnp.einsum("td,tce->dce", ln1_low, back_qkv, preferred_element_type=jnp.float32)

    def qkv_back_term(start, count):
        return jnp.einsum("tce,dce->td", back_qkv, w_qkv, preferred_element_type=jnp.float32)

    back_ln1 = sum_over_mp(qkv_back_term)
    ln1_again, ln1_back = jax.vjp(layer_norm, x_in, norm_full[:, 0], norm_full[:, 1])
    back_input, gain1_sum, shift1_sum = ln1_back(back_ln1)
    whole = back_resid_part + back_input
    norm_part = jnp.stack(
        [
            gain1_sum,
            shift1_sum,
            gain2_sum,
            shift2_sum,
            jnp.sum(back_resid_part, axis=0),
            jnp.sum(upstream, axis=0),
        ],
        axis=1,
    )
    qkv_reduced, proj_reduced, fc_reduced, down_reduced, norm_reduced = (
        lax.psum_scatter(qkv_sum, "dp", scatter_dimension=0, tiled=True),
        lax.psum_scatter(proj_sum, "dp", scatter_dimension=0, tiled=True),
        lax.psum_scatter(fc_sum, "dp", scatter_dimension=0, tiled=True),
        lax.psum_scatter(down_sum, "dp", scatter_dimension=0, tiled=True),
        lax.psum_scatter(norm_part, "dp", scatter_dimension=0, tiled=True),
    )
    attn_bias_reduced, fc_bias_reduced = lax.psum((attn_bias_sum, fc_bias_sum), "dp")
    raw_grads = [
        reduced / valid_total
        for reduced in (
            norm_reduced,
            attn_bias_reduced,
            qkv_reduced,
            proj_reduced,
            fc_bias_reduced,
            fc_reduced,
            down_reduced,
        )
    ]
    local_squares = jnp.sum(raw_grads[0] * raw_grads[0]) / float(mp_count)
    local_squares = local_squares + jnp.sum(raw_grads[1] * raw_grads[1]) / float(dp_count)
    local_squares = local_squares + jnp.sum(raw_grads[4] * raw_grads[4]) / float(dp_count)
    for grad_raw in (raw_grads[2], raw_grads[3], raw_grads[5], raw_grads[6]):
        local_squares = local_squares + jnp.sum(grad_raw * grad_raw)
    squares = lax.psum(local_squares, ("dp", "mp"))
    grad_norm = jnp.sqrt(squares)
    clip_factor = jnp.minimum(1.0, 1.0 / (grad_norm + 1e-06))
    masters = (
        norm_master,
        attn_bias_master,
        qkv_master,
        proj_master,
        fc_bias_master,
        fc_master,
        down_master,
    )
    moments = (
        norm_moment,
        attn_bias_moment,
        qkv_moment,
        proj_moment,
        fc_bias_moment,
        fc_moment,
        down_moment,
    )
    averages = (
        norm_average,
        attn_bias_average,
        qkv_average,
        proj_average,
        fc_bias_average,
        fc_average,
        down_average,
    )
    grads_out = []
    momenta_out = []
    averaged_out = []
    updated_out = []
    copies_out = []
    for master, moment, average, grad_raw in zip(masters, moments, averages, raw_grads):
        clipped = grad_raw * clip_factor
        momentum = MOMENTUM * moment + clipped
        updated = master - RATE * (clipped + MOMENTUM * momentum)
        averaged = KEEP * average + (1.0 - KEEP) * updated
        grads_out.append(clipped)
        momenta_out.append(momentum)
        averaged_out.append(averaged)
        updated_out.append(updated)
        copies_out.append(updated.astype(jnp.bfloat16))
    return (
        block_part,
        whole,
        grads_out[0],
        grads_out[1],
        grads_out[2],
        grads_out[3],
        grads_out[4],
        grads_out[5],
        grads_out[6],
        momenta_out[0],
        momenta_out[1],
        momenta_out[2],
        momenta_out[3],
        momenta_out[4],
        momenta_out[5],
        momenta_out[6],
        averaged_out[0],
        averaged_out[1],
        averaged_out[2],
        averaged_out[3],
        averaged_out[4],
        averaged_out[5],
        averaged_out[6],
        updated_out[0],
        updated_out[1],
        updated_out[2],
        updated_out[3],
        updated_out[4],
        updated_out[5],
        updated_out[6],
        copies_out[0],
        copies_out[1],
        copies_out[2],
        copies_out[3],
        copies_out[4],
        copies_out[5],
        copies_out[6],
        grad_norm,
    )


def solution(mesh):
    placed = (
        P("dp", None),
        P("dp", None),
        P("dp"),
        P("dp", None),
        P(),
        P("dp", None),
        P(None, "mp"),
        P("dp", None, "mp"),
        P("dp", "mp"),
        P("mp"),
        P("dp", "mp"),
        P("dp", "mp"),
        P("dp", None),
        P(None, "mp"),
        P("dp", None, "mp"),
        P("dp", "mp"),
        P("mp"),
        P("dp", "mp"),
        P("dp", "mp"),
        P("dp", None),
        P(None, "mp"),
        P("dp", None, "mp"),
        P("dp", "mp"),
        P("mp"),
        P("dp", "mp"),
        P("dp", "mp"),
    )
    return jax.shard_map(
        local,
        mesh=mesh,
        in_specs=placed,
        out_specs=(
            P("dp", None),
            P("dp", None),
            P("dp", None),
            P(None, "mp"),
            P("dp", None, "mp"),
            P("dp", "mp"),
            P("mp"),
            P("dp", "mp"),
            P("dp", "mp"),
            P("dp", None),
            P(None, "mp"),
            P("dp", None, "mp"),
            P("dp", "mp"),
            P("mp"),
            P("dp", "mp"),
            P("dp", "mp"),
            P("dp", None),
            P(None, "mp"),
            P("dp", None, "mp"),
            P("dp", "mp"),
            P("mp"),
            P("dp", "mp"),
            P("dp", "mp"),
            P("dp", None),
            P(None, "mp"),
            P("dp", None, "mp"),
            P("dp", "mp"),
            P("mp"),
            P("dp", "mp"),
            P("dp", "mp"),
            P("dp", None),
            P(None, "mp"),
            P("dp", None, "mp"),
            P("dp", "mp"),
            P("mp"),
            P("dp", "mp"),
            P("dp", "mp"),
            P(),
        ),
        check_vma=False,
    )
```

profile of v0, /device:TPU:0, one launch (start us, length us, event | category | flops | bytes accessed | tf_op | source)
XLA Modules:
  0.0 2152.3 jit_solution(12280135592228971859)
XLA Ops:
  15.6 3.4 fusion.15
  19.1 32.9 %all_gather.15 = bf16[2048,6]{0,1:T(8,128)(2,1)S(1)} all-gather(bf16[256,6]{0,1:T(8,128)(2,1)S(1)} %convert_element_type.108), channel_id=1, replica_groups=mesh['dp'=8,'mp'=4] {'dp'}, dimensions={0}, use_global_device_ids=true | all-gather | bytes 27648 | tf_op jit(solution)/shard_map/all_gather | solution.py:96
  52.7 61.0 %all-gather.5.cloned.1.call-done = bf16[2048,3,512]{0,2,1:T(8,128)(2,1)} async-done(((bf16[256,3,512]{0,2,1:T(8,128)(2,1)}), bf16[2048,3,512]{0,2,1:T(8,128)(2,1)}) %all-gather.5.cloned.1.call-update) | async-done | bytes 6291472 | tf_op jit(solution)/shard_map/all_gather | solution.py:92
  113.7 11.1 add_convert_fusion.2
  124.9 3.3 fusion
  128.3 3.7 exponential_reduce_fusion
  134.0 6.5 convolution_convert_fusion.1
  140.5 23.5 %all-gather.7.cloned.1.call-done = bf16[2048,512]{1,0:T(8,128)(2,1)} async-done(((bf16[256,512]{1,0:T(8,128)(2,1)}), bf16[2048,512]{1,0:T(8,128)(2,1)}) %all-gather.7.cloned.1.call-update) | async-done | bytes 2097168 | tf_op jit(solution)/shard_map/all_gather | solution.py:93
  164.0 7.4 fusion.66
  174.3 3.2 convert_element_type.120
  178.8 18.5 psum.58
  201.1 121.8 %all-reduce.6.cloned.1.call-done = f32[1024,2048]{1,0:T(8,128)} async-done(((f32[1024,2048]{1,0:T(8,128)}), f32[1024,2048]{1,0:T(8,128)}) %all-reduce.6.cloned.1.call-update) | async-done | bytes 8388624 | tf_op jit(solution)/shard_map/psum | solution.py:70
  322.9 5.8 fusion.62
  328.7 3.3 copy-done
  333.0 117.6 %all-gather.9.cloned.1.call-done = bf16[2048,2048]{1,0:T(8,128)(2,1)} async-done(((bf16[256,2048]{1,0:T(8,128)(2,1)}), bf16[2048,2048]{1,0:T(8,128)(2,1)}) %all-gather.9.cloned.1.call-update) | async-done | bytes 8388624 | tf_op jit(solution)/shard_map/all_gather | solution.py:94
  450.6 15.9 fusion.51
  466.5 109.8 %all-gather.11.cloned.1.call-done = bf16[2048,2048]{1,0:T(8,128)(2,1)} async-done(((bf16[256,2048]{1,0:T(8,128)(2,1)}), bf16[2048,2048]{1,0:T(8,128)(2,1)}) %all-gather.11.cloned.1.call-update) | async-done | bytes 8388624 | tf_op jit(solution)/shard_map/all_gather | solution.py:95
  576.3 21.0 convert_reduce_fusion.1
  599.2 11.1 fusion.67
  610.3 18.3 fusion.49
  628.6 132.9 %all-reduce.8.cloned.1.call-done = f32[1024,2048]{1,0:T(8,128)} async-done(((f32[1024,2048]{1,0:T(8,128)}), f32[1024,2048]{1,0:T(8,128)}) %all-reduce.8.cloned.1.call-update) | async-done | bytes 8388624 | tf_op jit(solution)/shard_map/psum | solution.py:70
  761.5 7.5 multiply_reduce_fusion.1
  769.7 5.0 fusion.61
  774.7 6.3 fusion.33
  781.1 9.7 convolution_convert_fusion
  790.7 12.6 multiply_reduce_fusion
  803.3 12.1 multiply_convert_fusion
  823.1 11.0 convolution_bitcast_fusion
  835.3 9.5 fusion.23
  844.9 278.3 %all-reduce.10.cloned.1.call-done = (f32[1024,2048]{1,0:T(8,128)}, f32[1024,2048]{1,0:T(8,128)}) async-done(((f32[1024,2048]{1,0:T(8,128)}, f32[1024,2048]{1,0:T(8,128)}), (f32[1024,2048]{1,0:T(8,128)}, f32[1024,2048]{1,0:T(8,128)})) %all-reduce.10.cloned.1.call-update) | async-done | bytes 16777232 | tf_op jit(solution)/shard_map/psum | solution.py:70
  1123.3 6.4 fusion.53
  1131.6 3.9 fusion.10
  1135.5 10.2 fusion.20
  1146.7 13.6 fusion.36
  1161.0 16.4 fusion.50
  1177.7 17.1 fusion.27
  1195.5 37.8 %all-reduce = (f32[2,512]{1,0:T(2,128)S(1)}, f32[2048]{0:T(1024)S(1)}) all-reduce(f32[2,512]{1,0:T(2,128)S(1)} %convert_reduce_fusion.2, f32[2048]{0:T(1024)S(1)} %copy-done.48), channel_id=1, replica_groups=mesh['dp'=8,'mp'=4] {'dp'}, use_global_device_ids=true, to_apply=%region_28.29 | all-reduce | flops 3072 | bytes 24576 | tf_op jit(solution)/shard_map/psum | solution.py:231
  1239.6 41.7 %reduce-scatter.6.cloned.1.call-done = f32[256,6]{0,1:T(8,128)} async-done(((f32[2048,6]{0,1:T(8,128)}), f32[256,6]{0,1:T(8,128)}) %reduce-scatter.6.cloned.1.call-update) | async-done | bytes 6160 | tf_op jit(solution)/shard_map/reduce_scatter | solution.py:229
  1283.9 208.1 %reduce-scatter.8.cloned.1.call-done = f32[256,3,512]{2,0,1:T(8,128)} async-done(((f32[2048,3,512]{2,0,1:T(8,128)}), f32[256,3,512]{2,0,1:T(8,128)}) %reduce-scatter.8.cloned.1.call-update) | async-done | bytes 1572880 | tf_op jit(solution)/shard_map/reduce_scatter | solution.py:225
  1496.3 280.9 %reduce-scatter.12.cloned.1.call-done = f32[256,2048]{1,0:T(8,128)} async-done(((f32[2048,2048]{1,0:T(8,128)}), f32[256,2048]{1,0:T(8,128)}) %reduce-scatter.12.cloned.1.call-update) | async-done | bytes 2097168 | tf_op jit(solution)/shard_map/reduce_scatter | solution.py:227
  1777.2 3.4 multiply_reduce_fusion.5
  1781.3 281.4 %reduce-scatter.14.cloned.1.call-done = f32[256,2048]{1,0:T(8,128)} async-done(((f32[2048,2048]{1,0:T(8,128)}), f32[256,2048]{1,0:T(8,128)}) %reduce-scatter.14.cloned.1.call-update) | async-done | bytes 2097168 | tf_op jit(solution)/shard_map/reduce_scatter | solution.py:228
  2062.7 3.4 multiply_reduce_fusion.4
  2066.9 10.2 add_convert_fusion
  2077.0 39.2 %psum.63 = f32[]{:T(128)} all-reduce(f32[]{:T(128)S(6)} %add.249), channel_id=1, replica_groups=mesh['dp'=8,'mp'=4] {'dp','mp'}, use_global_device_ids=true, to_apply=%region_41.42 | all-reduce | flops 1 | bytes 8 | tf_op jit(solution)/shard_map/psum | solution.py:249
  2122.0 3.2 fusion.57
  2127.5 5.9 fusion.58
  2135.1 5.1 fusion.54
  (190 shorter events, 57.0 us)
Async XLA Ops:
  7.2 11.8 copy-start.40
  7.2 106.5 %all-gather.5.cloned.1.call-start = ((), (), s32[]{:S(2)}) async-start(), calls=%async_computation.5 | async-start | bytes 7077888 | tf_op jit(solution)/shard_map/all_gather | solution.py:92
  9.9 154.1 %all-gather.7.cloned.1.call-start = ((), (), s32[]{:S(2)}) async-start(), calls=%async_computation.6 | async-start | bytes 2359296 | tf_op jit(solution)/shard_map/all_gather | solution.py:93
  11.7 311.2 %all-reduce.6.cloned.1.call-start = ((), (), s32[]{:S(2)}) async-start(), calls=%async_computation.7 | async-start | bytes 16777216 | tf_op jit(solution)/shard_map/psum | solution.py:70
  15.6 109.2 %copy-start.28 = (f32[1024]{0:T(1024)}, f32[1024]{0:T(1024)S(1)}, u32[]{:S(2)}) copy-start(f32[1024]{0:T(1024)S(1)} %broadcast_multiply_fusion.8) | copy-start | bytes 12292
  19.0 105.8 %copy-start.32 = (f32[1024]{0:T(1024)}, f32[1024]{0:T(1024)S(1)}, u32[]{:S(2)}) copy-start(f32[1024]{0:T(1024)S(1)} %fusion.15) | copy-start | bytes 12292
  19.1 105.8 %copy-start.30 = (f32[1024]{0:T(1024)}, f32[1024]{0:T(1024)S(1)}, u32[]{:S(2)}) copy-start(f32[1024]{0:T(1024)S(1)} %fusion.42) | copy-start | bytes 12292
  52.6 72.3 %copy-start.26 = (f32[2048,1]{0,1:T(1,128)}, f32[2048,1]{0,1:T(1,128)S(1)}, u32[]{:S(2)}) copy-start(f32[2048,1]{0,1:T(1,128)S(1)} %get-tuple-element.123) | copy-start | bytes 24580
  52.6 72.3 %copy-start.46 = (f32[2048,1]{0,1:T(1,128)}, f32[2048,1]{0,1:T(1,128)S(1)}, u32[]{:S(2)}) copy-start(f32[2048,1]{0,1:T(1,128)S(1)} %get-tuple-element.124) | copy-start | bytes 24580
  52.6 398.0 %copy-start.44 = (f32[2048,1]{0,1:T(1,128)}, f32[2048,1]{0,1:T(1,128)S(1)}, u32[]{:S(2)}) copy-start(f32[2048,1]{0,1:T(1,128)S(1)} %get-tuple-element.121) | copy-start | bytes 24580
  140.4 31.0 %copy-start.56 = (bf16[4,128,1024]{2,1,0:T(8,128)(2,1)}, bf16[4,128,1024]{2,1,0:T(8,128)(2,1)S(1)}, u32[]{:S(2)}) copy-start(bf16[4,128,1024]{2,1,0:T(8,128)(2,1)S(1)} %convolution_convert_fusion.1) | copy-start | bytes 3145732
  171.4 25.9 %copy-start.54 = (s32[4]{0:T(128)S(1)}, s32[4]{0:T(128)}, u32[]{:S(2)}) copy-start(s32[4]{0:T(128)} %param.30) | copy-start | bytes 52
  171.4 279.2 %all-gather.9.cloned.1.call-start = ((), (), s32[]{:S(2)}) async-start(), calls=%async_computation.8 | async-start | bytes 9437184 | tf_op jit(solution)/shard_map/all_gather | solution.py:94
  174.2 402.1 %all-gather.11.cloned.1.call-start = ((), (), s32[]{:S(2)}) async-start(), calls=%async_computation.9 | async-start | bytes 9437184 | tf_op jit(solution)/shard_map/all_gather | solution.py:95
  177.5 584.0 %all-reduce.8.cloned.1.call-start = ((), (), s32[]{:S(2)}) async-start(), calls=%async_computation.10 | async-start | bytes 16777216 | tf_op jit(solution)/shard_map/psum | solution.py:70
  450.6 125.7 %copy-start.49 = (f32[2048]{0:T(1024)S(1)}, f32[2048]{0:T(1024)}, u32[]{:S(2)}) copy-start(f32[2048]{0:T(1024)} %param.35) | copy-start | bytes 24580
  576.3 22.9 %copy-start.55 = (bf16[2048,2048]{1,0:T(8,128)(2,1)S(1)}, bf16[2048,2048]{1,0:T(8,128)(2,1)}, u32[]{:S(2)}) copy-start(bf16[2048,2048]{1,0:T(8,128)(2,1)} %all-gather.9.cloned.1.call-done) | copy-start | bytes 25165828
  610.3 513.0 %all-reduce.10.cloned.1.call-start = ((), (), s32[]{:S(2)}) async-start(), calls=%async_computation.16 | async-start | bytes 33554432 | tf_op jit(solution)/shard_map/psum | solution.py:70
  834.1 289.2 %copy-start.27 = (f32[2048,1]{0,1:T(1,128)S(1)}, f32[2048,1]{0,1:T(1,128)}, u32[]{:S(2)}) copy-start(f32[2048,1]{0,1:T(1,128)} %copy-done.26) | copy-start | bytes 24580
  834.1 289.1 %copy-start.29 = (f32[1024]{0:T(1024)S(1)}, f32[1024]{0:T(1024)}, u32[]{:S(2)}) copy-start(f32[1024]{0:T(1024)} %copy-done.28) | copy-start | bytes 12292
  834.1 403.0 %reduce-scatter.10.cloned.1.call-start = ((), (), s32[]{:S(2)}) async-start(), calls=%async_computation.13 | async-start | bytes 4718592 | tf_op jit(solution)/shard_map/reduce_scatter | solution.py:226
  844.8 284.8 %copy-start.33 = (f32[1024]{0:T(1024)S(1)}, f32[1024]{0:T(1024)}, u32[]{:S(2)}) copy-start(f32[1024]{0:T(1024)} %copy-done.32) | copy-start | bytes 12292
  844.8 284.8 %copy-start.31 = (f32[1024]{0:T(1024)S(1)}, f32[1024]{0:T(1024)}, u32[]{:S(2)}) copy-start(f32[1024]{0:T(1024)} %copy-done.30) | copy-start | bytes 12292
  844.9 436.4 %reduce-scatter.6.cloned.1.call-start = ((), (), s32[]{:S(2)}) async-start(), calls=%async_computation.11 | async-start | bytes 73728 | tf_op jit(solution)/shard_map/reduce_scatter | solution.py:229
  1135.5 11.2 copy-start.17
  1135.5 11.2 copy-start.47
  1146.5 345.5 %reduce-scatter.8.cloned.1.call-start = ((), (), s32[]{:S(2)}) async-start(), calls=%async_computation.12 | async-start | bytes 14155776 | tf_op jit(solution)/shard_map/reduce_scatter | solution.py:225
  1160.3 616.9 %reduce-scatter.12.cloned.1.call-start = ((), (), s32[]{:S(2)}) async-start(), calls=%async_computation.14 | async-start | bytes 18874368 | tf_op jit(solution)/shard_map/reduce_scatter | solution.py:227
  1177.4 885.3 %reduce-scatter.14.cloned.1.call-start = ((), (), s32[]{:S(2)}) async-start(), calls=%async_computation.15 | async-start | bytes 18874368 | tf_op jit(solution)/shard_map/reduce_scatter | solution.py:228
  1194.8 871.9 %copy-start.34 = (f32[2048,1]{0,1:T(1,128)S(1)}, f32[2048,1]{0,1:T(1,128)}, u32[]{:S(2)}) copy-start(f32[2048,1]{0,1:T(1,128)} %get-tuple-element.119) | copy-start | bytes 24580
  2066.7 50.2 %copy-start.50 = (f32[2048]{0:T(1024)S(1)}, f32[2048]{0:T(1024)}, u32[]{:S(2)}) copy-start(f32[2048]{0:T(1024)} %param.42) | copy-start | bytes 24580
  2066.8 51.6 %copy-start.41 = (f32[2,512]{1,0:T(2,128)S(1)}, f32[2,512]{1,0:T(2,128)}, u32[]{:S(2)}) copy-start(f32[2,512]{1,0:T(2,128)} %param.32) | copy-start | bytes 12292
  2066.8 51.6 %copy-start.53 = (f32[2,512]{1,0:T(2,128)S(1)}, f32[2,512]{1,0:T(2,128)}, u32[]{:S(2)}) copy-start(f32[2,512]{1,0:T(2,128)} %param.39) | copy-start | bytes 12292
  2066.8 52.2 %copy-start.52 = (f32[2,512]{1,0:T(2,128)S(1)}, f32[2,512]{1,0:T(2,128)}, u32[]{:S(2)}) copy-start(f32[2,512]{1,0:T(2,128)} %param.46) | copy-start | bytes 12292
  2066.8 52.7 %copy-start.42 = (f32[2048]{0:T(1024)S(1)}, f32[2048]{0:T(1024)}, u32[]{:S(2)}) copy-start(f32[2048]{0:T(1024)} %param.49) | copy-start | bytes 24580
  2066.8 53.3 %copy-start.37 = (f32[256,6]{0,1:T(8,128)S(1)}, f32[256,6]{0,1:T(8,128)}, u32[]{:S(2)}) copy-start(f32[256,6]{0,1:T(8,128)} %param.31) | copy-start | bytes 18436
  2066.8 53.3 %copy-start.38 = (f32[256,6]{0,1:T(8,128)S(1)}, f32[256,6]{0,1:T(8,128)}, u32[]{:S(2)}) copy-start(f32[256,6]{0,1:T(8,128)} %reduce-scatter.6.cloned.1.call-done) | copy-start | bytes 18436
  2066.8 53.3 %copy-start.51 = (f32[256,6]{0,1:T(8,128)S(1)}, f32[256,6]{0,1:T(8,128)}, u32[]{:S(2)}) copy-start(f32[256,6]{0,1:T(8,128)} %param.38) | copy-start | bytes 18436
  2066.8 54.6 %copy-start.43 = (f32[256,6]{0,1:T(8,128)S(1)}, f32[256,6]{0,1:T(8,128)}, u32[]{:S(2)}) copy-start(f32[256,6]{0,1:T(8,128)} %param.45) | copy-start | bytes 18436
  2066.9 60.6 %copy-start.12 = (f32[256,3,512]{2,0,1:T(8,128)S(1)}, f32[256,3,512]{2,0,1:T(8,128)}, u32[]{:S(2)}) copy-start(f32[256,3,512]{2,0,1:T(8,128)} %param.33) | copy-start | bytes 4718596
  2066.9 60.6 %copy-start.13 = (f32[256,3,512]{2,0,1:T(8,128)S(1)}, f32[256,3,512]{2,0,1:T(8,128)}, u32[]{:S(2)}) copy-start(f32[256,3,512]{2,0,1:T(8,128)} %reduce-scatter.8.cloned.1.call-done) | copy-start | bytes 4718596
  2116.9 16.5 copy-start.25
  2118.3 16.7 copy-start.35
  2118.9 16.1 copy-start.39
  2121.4 13.7 copy-start.36
  2125.3 15.0 copy-start.22
  2125.3 9.8 copy-start.11
  2125.3 9.8 copy-start.23
  (23 other events, 132.8 us)
Sparse Core Ops, SparseCore 0:
  10.7 102.9 all-gather.4
  116.4 47.5 all-gather.6
  171.5 151.3 all-reduce.5
  325.5 125.0 all-gather.8
  453.1 123.1 all-gather.10
  610.4 151.0 all-reduce.7
  834.2 288.9 all-reduce.9
  1127.5 88.2 reduce-scatter.9
  1220.1 61.1 reduce-scatter.5
  1285.1 206.7 reduce-scatter.7
  1496.2 280.9 reduce-scatter.11
  1780.9 281.7 reduce-scatter.13
where the time goes:
time: 2160 us; the launch traced here: 2150 us
  waiting for transfers between devices  1660 us (77%)
  matrix products  195 us (9%)
  other arithmetic  128 us (6%)
  blocking collectives  128 us (6%)
  between operations  23.6 us (1%)
    psum x3, waiting for transfers between devices, sum_over_mp(): summed = lax.psum(term_fn(0, row_count), 'mp')  533 us
    reduce_scatter x1, waiting for transfers between devices, local(): lax.psum_scatter(down_sum, 'dp', scatter_dimension=0, tiled=True)  281 us
    reduce_scatter x1, waiting for transfers between devices, local(): lax.psum_scatter(fc_sum, 'dp', scatter_dimension=0, tiled=True)  281 us
    reduce_scatter x1, waiting for transfers between devices, local(): lax.psum_scatter(qkv_sum, 'dp', scatter_dimension=0, tiled=True)  208 us
    all_gather x1, waiting for transfers between devices, local(): lax.all_gather(low_fc, 'dp', axis=0, tiled=True)  118 us
    all_gather x1, waiting for transfers between devices, local(): lax.all_gather(low_down, 'dp', axis=0, tiled=True)  110 us
    all_gather x1, waiting for transfers between devices, local(): lax.all_gather(low_qkv, 'dp', axis=0, tiled=True)  61 us
  transfers between devices with their start and end apart: 12, of which 11 were waited for; matrix products, arithmetic and copies ran while one was open for 8% of the time, Pallas kernels for 0%

commit v1 on v0

--- a/solution.py
+++ b/solution.py
@@ -67,7 +67,9 @@
     dp_count = lax.axis_size("dp")
 
     def sum_over_mp(term_fn):
-        summed = lax.psum(term_fn(0, row_count), "mp")
+        part = term_fn(0, row_count)
+        shards = lax.all_gather(part, "mp", axis=0, tiled=False)
+        summed = shards.sum(axis=0)
         return summed
 
     family_ids = jnp.arange(family_count, dtype=jnp.int32)

time: 2160 us -> 2270 us (1.051)
  other arithmetic: 128 us -> 218 us
    all_gather x0 -> x4, waiting for transfers between devices: none -> 684 us  [sum_over_mp(): shards = lax.all_gather(part, 'mp', axis=0, tiled=False)]
    psum x3 -> x0, waiting for transfers between devices: 533 us -> none  [sum_over_mp(): summed = lax.psum(term_fn(0, row_count), 'mp')]
    reduce_scatter x1, waiting for transfers between devices: 281 us -> 157 us  [local(): lax.psum_scatter(fc_sum, 'dp', scatter_dimension=0, tiled=True)]
    reduce_sum x0 -> x4, other arithmetic: none -> 71.5 us  [sum_over_mp(): summed = shards.sum(axis=0)]
    reduce_scatter x1, waiting for transfers between devices: 208 us -> 158 us  [local(): lax.psum_scatter(qkv_sum, 'dp', scatter_dimension=0, tiled=True)]
    reduce_scatter x1, waiting for transfers between devices: 0.02 us -> 32.9 us  [local(): lax.psum_scatter(proj_sum, 'dp', scatter_dimension=0, tiled=True)]
    reduce_sum x3 -> x5, other arithmetic: 17.7 us -> 43.3 us  [layer_norm(): return centred * lax.rsqrt(spread + EPS) * gain + shift]
  transfers between devices with their start and end apart: 12 -> 13, of which waited for: 11 -> 13; matrix products, arithmetic and copies ran while one was open for 8% -> 16% of each run, Pallas kernels for 0% -> 0%
where the time goes in v1:
time: 2270 us
  waiting for transfers between devices  1670 us (74%)
  other arithmetic  218 us (10%)
  matrix products  202 us (9%)
  blocking collectives  129 us (6%)
  local copies, waits for them, and re-layouts  26.1 us (1%)
  between operations  23.4 us (1%)
    all_gather x4, waiting for transfers between devices, sum_over_mp(): shards = lax.all_gather(part, 'mp', axis=0, tiled=False)  684 us
    reduce_scatter x1, waiting for transfers between devices, local(): lax.psum_scatter(down_sum, 'dp', scatter_dimension=0, tiled=True)  283 us
    reduce_scatter x1, waiting for transfers between devices, local(): lax.psum_scatter(qkv_sum, 'dp', scatter_dimension=0, tiled=True)  158 us
    reduce_scatter x1, waiting for transfers between devices, local(): lax.psum_scatter(fc_sum, 'dp', scatter_dimension=0, tiled=True)  157 us
    all_gather x1, waiting for transfers between devices, local(): lax.all_gather(low_down, 'dp', axis=0, tiled=True)  110 us
    all_gather x1, waiting for transfers between devices, local(): lax.all_gather(low_fc, 'dp', axis=0, tiled=True)  100 us
    reduce_sum x4, other arithmetic, sum_over_mp(): summed = shards.sum(axis=0)  71.5 us
    reduce_scatter x1, waiting for transfers between devices, local(): lax.psum_scatter(norm_part, 'dp', scatter_dimension=0, tiled=True)  61.7 us
  transfers between devices with their start and end apart: 13, of which 13 were waited for; matrix products, arithmetic and copies ran while one was open for 16% of the time, Pallas kernels for 0%

profile of v1, /device:TPU:0, one launch (start us, length us, event | category | flops | bytes accessed | tf_op | source)
XLA Modules:
  0.0 2269.3 jit_solution(2571759897764088357)
XLA Ops:
  19.1 32.9 %all_gather.39 = bf16[2048,6]{0,1:T(8,128)(2,1)S(1)} all-gather(bf16[256,6]{0,1:T(8,128)(2,1)S(1)} %convert_element_type.108), channel_id=1, replica_groups=mesh['dp'=8,'mp'=4] {'dp'}, dimensions={0}, use_global_device_ids=true | all-gather | bytes 27648 | tf_op jit(solution)/shard_map/all_gather | solution.py:98
  52.8 60.9 %all-gather.13.cloned.1.call-done = bf16[2048,3,512]{0,2,1:T(8,128)(2,1)} async-done(((bf16[256,3,512]{0,2,1:T(8,128)(2,1)}), bf16[2048,3,512]{0,2,1:T(8,128)(2,1)}) %all-gather.13.cloned.1.call-update) | async-done | bytes 6291472 | tf_op jit(solution)/shard_map/all_gather | solution.py:94
  113.7 11.1 add_convert_fusion.2
  134.0 6.5 convolution_convert_fusion.1
  140.5 23.4 %all-gather.15.cloned.1.call-done = bf16[2048,512]{1,0:T(8,128)(2,1)} async-done(((bf16[256,512]{1,0:T(8,128)(2,1)}), bf16[2048,512]{1,0:T(8,128)(2,1)}) %all-gather.15.cloned.1.call-update) | async-done | bytes 2097168 | tf_op jit(solution)/shard_map/all_gather | solution.py:95
  163.9 7.5 fusion.65
  175.5 196.1 %all-gather.21.cloned.1.call-done = f32[4096,2048]{1,0:T(8,128)} async-done(((f32[1024,2048]{1,0:T(8,128)}), f32[4096,2048]{1,0:T(8,128)}) %all-gather.21.cloned.1.call-update) | async-done | bytes 33554448 | tf_op jit(solution)/shard_map/all_gather | solution.py:71
  371.6 16.7 reduce_sum.290
  388.3 5.8 fusion.61
  399.1 100.1 %all-gather.17.cloned.1.call-done = bf16[2048,2048]{1,0:T(8,128)(2,1)} async-done(((bf16[256,2048]{1,0:T(8,128)(2,1)}), bf16[2048,2048]{1,0:T(8,128)(2,1)}) %all-gather.17.cloned.1.call-update) | async-done | bytes 8388624 | tf_op jit(solution)/shard_map/all_gather | solution.py:96
  499.2 15.8 fusion.51
  514.9 109.9 %all-gather.19.cloned.1.call-done = bf16[2048,2048]{1,0:T(8,128)(2,1)} async-done(((bf16[256,2048]{1,0:T(8,128)(2,1)}), bf16[2048,2048]{1,0:T(8,128)(2,1)}) %all-gather.19.cloned.1.call-update) | async-done | bytes 8388624 | tf_op jit(solution)/shard_map/all_gather | solution.py:97
  624.9 17.3 fusion.49
  643.5 18.8 psum.28
  666.1 21.4 convert_reduce_fusion.1
  689.5 13.3 fusion.66
  702.8 16.8 fusion.50
  719.7 16.9 fusion.27
  736.6 105.4 %all-gather.23.cloned.1.call-done = f32[4096,2048]{1,0:T(8,128)} async-done(((f32[1024,2048]{1,0:T(8,128)}), f32[4096,2048]{1,0:T(8,128)}) %all-gather.23.cloned.1.call-update) | async-done | bytes 33554448 | tf_op jit(solution)/shard_map/all_gather | solution.py:71
  842.0 21.1 reduce_sum.296
  863.1 182.1 %all-gather.25.cloned.1.call-done = f32[4096,2048]{1,0:T(8,128)} async-done(((f32[1024,2048]{1,0:T(8,128)}), f32[4096,2048]{1,0:T(8,128)}) %all-gather.25.cloned.1.call-update) | async-done | bytes 33554448 | tf_op jit(solution)/shard_map/all_gather | solution.py:71
  1045.1 16.7 reduce_sum.344
  1061.9 7.4 multiply_reduce_fusion.1
  1070.3 9.0 fusion.60
  1082.6 7.7 fusion.23
  1090.4 8.5 fusion.33
  1098.9 9.0 convolution_convert_fusion
  1108.5 12.9 multiply_reduce_fusion
  1121.4 12.8 multiply_convert_fusion
  1140.6 6.7 multiply_convert_fusion.2
  1148.7 11.2 convolution_bitcast_fusion
  1161.1 13.5 fusion.36
  1174.7 157.0 %reduce-scatter.12.cloned.1.call-done = f32[256,2048]{1,0:T(8,128)} async-done(((f32[2048,2048]{1,0:T(8,128)}), f32[256,2048]{1,0:T(8,128)}) %reduce-scatter.12.cloned.1.call-update) | async-done | bytes 2097168 | tf_op jit(solution)/shard_map/reduce_scatter | solution.py:229
  1335.1 282.7 %reduce-scatter.14.cloned.1.call-done = f32[256,2048]{1,0:T(8,128)} async-done(((f32[2048,2048]{1,0:T(8,128)}), f32[256,2048]{1,0:T(8,128)}) %reduce-scatter.14.cloned.1.call-update) | async-done | bytes 2097168 | tf_op jit(solution)/shard_map/reduce_scatter | solution.py:230
  1621.8 36.9 %all-reduce = (f32[2,512]{1,0:T(2,128)S(1)}, f32[2048]{0:T(1024)S(1)}) all-reduce(f32[2,512]{1,0:T(2,128)S(1)} %convert_reduce_fusion.2, f32[2048]{0:T(1024)S(1)} %copy-done.54), channel_id=1, replica_groups=mesh['dp'=8,'mp'=4] {'dp'}, use_global_device_ids=true, to_apply=%region_28.29 | all-reduce | flops 3072 | bytes 24576 | tf_op jit(solution)/shard_map/psum | solution.py:233
  1662.6 13.3 reduce_sum.354
  1675.9 32.9 %reduce-scatter.10.cloned.1.call-done = f32[256,512]{1,0:T(8,128)} async-done(((f32[2048,512]{1,0:T(8,128)}), f32[256,512]{1,0:T(8,128)}) %reduce-scatter.10.cloned.1.call-update) | async-done | bytes 524304 | tf_op jit(solution)/shard_map/reduce_scatter | solution.py:228
  1711.2 200.5 %all-gather.27.cloned.1.call-done = f32[4096,2048]{1,0:T(8,128)} async-done(((f32[1024,2048]{1,0:T(8,128)}), f32[4096,2048]{1,0:T(8,128)}) %all-gather.27.cloned.1.call-update) | async-done | bytes 33554448 | tf_op jit(solution)/shard_map/all_gather | solution.py:71
  1911.7 17.0 reduce_sum.348
  1928.7 13.0 reduce_sum.352
  1941.8 5.7 fusion.16
  1950.3 3.9 fusion.10
  1954.4 10.3 fusion.20
  1965.4 158.0 %reduce-scatter.8.cloned.1.call-done = f32[256,3,512]{2,0,1:T(8,128)} async-done(((f32[2048,3,512]{2,0,1:T(8,128)}), f32[256,3,512]{2,0,1:T(8,128)}) %reduce-scatter.8.cloned.1.call-update) | async-done | bytes 1572880 | tf_op jit(solution)/shard_map/reduce_scatter | solution.py:227
  2126.4 61.7 %reduce-scatter.6.cloned.1.call-done = f32[256,6]{0,1:T(8,128)} async-done(((f32[2048,6]{0,1:T(8,128)}), f32[256,6]{0,1:T(8,128)}) %reduce-scatter.6.cloned.1.call-update) | async-done | bytes 6160 | tf_op jit(solution)/shard_map/reduce_scatter | solution.py:231
  2193.3 40.4 %psum.31 = f32[]{:T(128)} all-reduce(f32[]{:T(128)S(6)} %add.241), channel_id=1, replica_groups=mesh['dp'=8,'mp'=4] {'dp','mp'}, use_global_device_ids=true, to_apply=%region_41.42 | all-reduce | flops 1 | bytes 8 | tf_op jit(solution)/shard_map/psum | solution.py:251
  2244.3 6.4 fusion.57
  2252.5 5.1 fusion.53
  (208 shorter events, 86.2 us)
Async XLA Ops:
  7.2 11.9 copy-start.48
  7.2 106.5 %all-gather.13.cloned.1.call-start = ((), (), s32[]{:S(2)}) async-start(), calls=%async_computation.5 | async-start | bytes 7077888 | tf_op jit(solution)/shard_map/all_gather | solution.py:94
  9.9 154.1 %all-gather.15.cloned.1.call-start = ((), (), s32[]{:S(2)}) async-start(), calls=%async_computation.6 | async-start | bytes 2359296 | tf_op jit(solution)/shard_map/all_gather | solution.py:95
  11.7 359.9 %all-gather.21.cloned.1.call-start = ((), (), s32[]{:S(2)}) async-start(), calls=%async_computation.14 | async-start | bytes 41943040 | tf_op jit(solution)/shard_map/all_gather | solution.py:71
  12.1 119.9 %copy-start.7 = (pred[1024,1024]{0,1:T(8,128)(4,1)}, pred[1024,1024]{0,1:T(8,128)(4,1)S(1)}, u32[]{:S(2)}) copy-start(pred[1024,1024]{0,1:T(8,128)(4,1)S(1)} %iota_compare_fusion) | copy-start | bytes 3145732
  15.6 109.2 %copy-start.35 = (f32[1024]{0:T(1024)}, f32[1024]{0:T(1024)S(1)}, u32[]{:S(2)}) copy-start(f32[1024]{0:T(1024)S(1)} %broadcast_multiply_fusion.8) | copy-start | bytes 12292
  19.1 105.8 %copy-start.41 = (f32[1024]{0:T(1024)}, f32[1024]{0:T(1024)S(1)}, u32[]{:S(2)}) copy-start(f32[1024]{0:T(1024)S(1)} %fusion.15) | copy-start | bytes 12292
  19.1 105.8 %copy-start.39 = (f32[1024]{0:T(1024)}, f32[1024]{0:T(1024)S(1)}, u32[]{:S(2)}) copy-start(f32[1024]{0:T(1024)S(1)} %fusion.42) | copy-start | bytes 12292
  52.6 72.3 %copy-start.33 = (f32[2048,1]{0,1:T(1,128)}, f32[2048,1]{0,1:T(1,128)S(1)}, u32[]{:S(2)}) copy-start(f32[2048,1]{0,1:T(1,128)S(1)} %get-tuple-element.119) | copy-start | bytes 24580
  52.6 72.3 %copy-start.52 = (f32[2048,1]{0,1:T(1,128)}, f32[2048,1]{0,1:T(1,128)S(1)}, u32[]{:S(2)}) copy-start(f32[2048,1]{0,1:T(1,128)S(1)} %get-tuple-element.120) | copy-start | bytes 24580
  140.5 31.0 %copy-start.62 = (bf16[4,128,1024]{2,1,0:T(8,128)(2,1)}, bf16[4,128,1024]{2,1,0:T(8,128)(2,1)S(1)}, u32[]{:S(2)}) copy-start(bf16[4,128,1024]{2,1,0:T(8,128)(2,1)S(1)} %convolution_convert_fusion.1) | copy-start | bytes 3145732
  171.5 327.7 %all-gather.17.cloned.1.call-start = ((), (), s32[]{:S(2)}) async-start(), calls=%async_computation.7 | async-start | bytes 9437184 | tf_op jit(solution)/shard_map/all_gather | solution.py:96
  172.7 452.2 %all-gather.19.cloned.1.call-start = ((), (), s32[]{:S(2)}) async-start(), calls=%async_computation.8 | async-start | bytes 9437184 | tf_op jit(solution)/shard_map/all_gather | solution.py:97
  175.5 666.5 %all-gather.23.cloned.1.call-start = ((), (), s32[]{:S(2)}) async-start(), calls=%async_computation.15 | async-start | bytes 41943040 | tf_op jit(solution)/shard_map/all_gather | solution.py:71
  499.2 125.7 %copy-start.55 = (f32[2048]{0:T(1024)S(1)}, f32[2048]{0:T(1024)}, u32[]{:S(2)}) copy-start(f32[2048]{0:T(1024)} %param.35) | copy-start | bytes 24580
  642.1 20.2 copy-start.61
  642.2 403.0 %all-gather.25.cloned.1.call-start = ((), (), s32[]{:S(2)}) async-start(), calls=%async_computation.16 | async-start | bytes 41943040 | tf_op jit(solution)/shard_map/all_gather | solution.py:71
  702.8 628.9 %reduce-scatter.12.cloned.1.call-start = ((), (), s32[]{:S(2)}) async-start(), calls=%async_computation.12 | async-start | bytes 18874368 | tf_op jit(solution)/shard_map/reduce_scatter | solution.py:229
  719.6 898.1 %reduce-scatter.14.cloned.1.call-start = ((), (), s32[]{:S(2)}) async-start(), calls=%async_computation.13 | async-start | bytes 18874368 | tf_op jit(solution)/shard_map/reduce_scatter | solution.py:230
  736.6 972.1 %reduce-scatter.10.cloned.1.call-start = ((), (), s32[]{:S(2)}) async-start(), calls=%async_computation.11 | async-start | bytes 4718592 | tf_op jit(solution)/shard_map/reduce_scatter | solution.py:228
  1090.3 821.4 %all-gather.27.cloned.1.call-start = ((), (), s32[]{:S(2)}) async-start(), calls=%async_computation.17 | async-start | bytes 41943040 | tf_op jit(solution)/shard_map/all_gather | solution.py:71
  1159.9 963.5 %reduce-scatter.8.cloned.1.call-start = ((), (), s32[]{:S(2)}) async-start(), calls=%async_computation.10 | async-start | bytes 14155776 | tf_op jit(solution)/shard_map/reduce_scatter | solution.py:227
  1174.6 447.2 %copy-start.54 = (f32[2048]{0:T(1024)S(1)}, f32[2048]{0:T(1024)}, u32[]{:S(2)}) copy-start(f32[2048]{0:T(1024)} %get-tuple-element.127) | copy-start | bytes 24580
  1174.6 1013.5 %reduce-scatter.6.cloned.1.call-start = ((), (), s32[]{:S(2)}) async-start(), calls=%async_computation.9 | async-start | bytes 73728 | tf_op jit(solution)/shard_map/reduce_scatter | solution.py:231
  1954.2 280.2 %copy-start.56 = (f32[2048]{0:T(1024)S(1)}, f32[2048]{0:T(1024)}, u32[]{:S(2)}) copy-start(f32[2048]{0:T(1024)} %param.35) | copy-start | bytes 24580
  1954.2 280.2 %copy-start.57 = (f32[2048]{0:T(1024)S(1)}, f32[2048]{0:T(1024)}, u32[]{:S(2)}) copy-start(f32[2048]{0:T(1024)} %param.42) | copy-start | bytes 24580
  1954.3 281.6 %copy-start.49 = (f32[2,512]{1,0:T(2,128)S(1)}, f32[2,512]{1,0:T(2,128)}, u32[]{:S(2)}) copy-start(f32[2,512]{1,0:T(2,128)} %param.32) | copy-start | bytes 12292
  1954.3 281.6 %copy-start.60 = (f32[2,512]{1,0:T(2,128)S(1)}, f32[2,512]{1,0:T(2,128)}, u32[]{:S(2)}) copy-start(f32[2,512]{1,0:T(2,128)} %param.39) | copy-start | bytes 12292
  1954.3 282.2 %copy-start.59 = (f32[2,512]{1,0:T(2,128)S(1)}, f32[2,512]{1,0:T(2,128)}, u32[]{:S(2)}) copy-start(f32[2,512]{1,0:T(2,128)} %param.46) | copy-start | bytes 12292
  1954.3 282.8 %copy-start.50 = (f32[2048]{0:T(1024)S(1)}, f32[2048]{0:T(1024)}, u32[]{:S(2)}) copy-start(f32[2048]{0:T(1024)} %param.49) | copy-start | bytes 24580
  1954.3 283.3 %copy-start.45 = (f32[256,6]{0,1:T(8,128)S(1)}, f32[256,6]{0,1:T(8,128)}, u32[]{:S(2)}) copy-start(f32[256,6]{0,1:T(8,128)} %param.31) | copy-start | bytes 18436
  1954.3 283.3 %copy-start.58 = (f32[256,6]{0,1:T(8,128)S(1)}, f32[256,6]{0,1:T(8,128)}, u32[]{:S(2)}) copy-start(f32[256,6]{0,1:T(8,128)} %param.38) | copy-start | bytes 18436
  1954.3 285.3 %copy-start.51 = (f32[256,6]{0,1:T(8,128)S(1)}, f32[256,6]{0,1:T(8,128)}, u32[]{:S(2)}) copy-start(f32[256,6]{0,1:T(8,128)} %param.45) | copy-start | bytes 18436
  1954.3 285.9 %copy-start.24 = (f32[256,512]{1,0:T(8,128)S(1)}, f32[256,512]{1,0:T(8,128)}, u32[]{:S(2)}) copy-start(f32[256,512]{1,0:T(8,128)} %param.34) | copy-start | bytes 1572868
  1954.4 285.9 %copy-start.25 = (f32[256,512]{1,0:T(8,128)S(1)}, f32[256,512]{1,0:T(8,128)}, u32[]{:S(2)}) copy-start(f32[256,512]{1,0:T(8,128)} %reduce-scatter.10.cloned.1.call-done) | copy-start | bytes 1572868
  1954.4 285.9 %copy-start.30 = (f32[256,512]{1,0:T(8,128)S(1)}, f32[256,512]{1,0:T(8,128)}, u32[]{:S(2)}) copy-start(f32[256,512]{1,0:T(8,128)} %param.41) | copy-start | bytes 1572868
  1954.4 289.9 %copy-start.16 = (f32[256,3,512]{2,0,1:T(8,128)S(1)}, f32[256,3,512]{2,0,1:T(8,128)}, u32[]{:S(2)}) copy-start(f32[256,3,512]{2,0,1:T(8,128)} %param.33) | copy-start | bytes 4718596
  2234.4 16.3 copy-start.28
  2235.8 16.6 copy-start.43
  2236.4 16.0 copy-start.47
  2239.6 12.8 copy-start.44
  2242.1 15.5 copy-start.23
  2242.1 10.3 copy-start.12
  2242.1 10.3 copy-start.13
  2242.1 10.3 copy-start.14
  2242.1 10.3 copy-start.15
  2242.1 10.3 copy-start.26
  2242.1 10.3 copy-start.27
  (29 other events, 146.1 us)
Sparse Core Ops, SparseCore 0:
  10.7 102.9 all-gather.12
  116.4 47.4 all-gather.14
  171.6 199.9 all-gather.20
  374.2 124.9 all-gather.16
  501.7 123.1 all-gather.18
  642.3 199.6 all-gather.22
  843.6 201.5 all-gather.24
  1048.9 282.7 reduce-scatter.11
  1336.0 281.7 reduce-scatter.13
  1621.2 87.4 reduce-scatter.9
  1710.4 201.2 all-gather.26
  1915.6 207.7 reduce-scatter.7
  2127.7 60.3 reduce-scatter.5
